TPU v7x, 32 devices: a whole 2x2x4 slice. The times are simulated.
32 devices in a mesh: cell: 4 (over y, x), sub: 8 (over z, core).
Axes of the slice: x: 2, y: 2, z: 4, core: 2. Of those that a mesh axis runs over, the one named last changes fastest.
Arguments:
- shell_conc: float32 [4, 32, 10, 128, 128], P('cell', 'sub'), may hold values from 0.2 to 0.8
- heat_rise: float32 [4, 30, 128, 128], P('cell', None, 'sub'), may hold values from -5 to 5
- layer_current: float32 [4, 32, 128, 128], P('cell', 'sub'), may hold values from -4 to 4
- layer_counts: int32 [8], replicated, may hold values from 1 to 4, 30 in all
- contacts: int32 [4, 2], replicated, may hold values from -1 to 3, as said below
Outputs:
- conc_new: float32 [4, 32, 10, 128, 128], P('cell', 'sub')
- heat_new: float32 [4, 30, 128, 128], P('cell', None, 'sub')
Inputs may be any that keep to these rules, and one draw needn't show every extreme that they name: `layer_counts`: entry d is the number of consecutive layers held by index d of sub, in order; the entries sum to 30 and the largest is exactly 4. `contacts`: row c names the cell below and the cell above cell c in one stacking order of all 4 cells, each cell once; -1 marks the two ends of the stack.
All inputs are finite; a program needn't handle non-finite values.
Results may differ from a plain program's by a relative error of at most 0.0003.
Values sent between devices are 32-bit elements; how exact they have to be, the bound alone decides.
A program may use at most 64 MiB of HBM per device.

v0:
```python
import functools

import jax
import jax.numpy as jnp
from jax import lax
from jax.experimental import pallas as pl
from jax.experimental.pallas import tpu as pltpu
from jax.sharding import PartitionSpec as P

BASE_KELVIN = 298.15
RATE_ACTIVATION = 5000.0
DIFFUSION_ACTIVATION = 3000.0
RATE_CONSTANT = 0.5
VOLT_PER_KELVIN = 2.0 * 8.314462618 / 96485.33212
HEAT_SCALE = 10.0
ENTROPY_SLOPE = 0.001
DIFFUSION_STEP = 0.005
SURFACE_STEP = 0.005
INPLANE_CONDUCT = 0.25
THROUGH_CONDUCT = 2.0
CONTACT_CONDUCT = 0.5
MESH = pl.DeviceIdType.MESH
GRANT = 24 << 20


def partner(me, offset):
    bit = 1
    result = me
    while bit <= offset:
        if offset & bit:
            result = result + bit * (1 - 2 * ((me // bit) % 2))
        bit *= 2
    return result


def peer_of(me, offset, count):
    if count & (count - 1) == 0:
        return partner(me, offset)
    return (me + offset) % count


def inverse_sine(value):
    magnitude = jnp.abs(value)
    rooted = jnp.sqrt(1.0 + magnitude * magnitude)
    positive = jnp.log1p(magnitude + magnitude * magnitude / (1.0 + rooted))
    return jnp.where(value < 0.0, -positive, positive), rooted


def kinetics(surface, rise, current):
    kelvin = BASE_KELVIN + rise
    per_kelvin = 1.0 / kelvin
    reciprocal = rise * (1.0 / BASE_KELVIN) * per_kelvin
    ratio_rate = (
        current
        * jnp.exp(-RATE_ACTIVATION * reciprocal)
        * lax.rsqrt(surface * (1.0 - surface))
        * (0.5 / RATE_CONSTANT)
    )
    arcsine, rooted = inverse_sine(ratio_rate)
    entropic = ENTROPY_SLOPE * (0.5 - surface)
    scaled = HEAT_SCALE * current
    common = VOLT_PER_KELVIN * arcsine + entropic
    source = scaled * kelvin * common
    heat_slope = scaled * (
        common - (VOLT_PER_KELVIN * RATE_ACTIVATION) * ratio_rate * per_kelvin / rooted
    )
    return source, heat_slope


def kernel(
    cells, subs,
    counts_hbm, contacts_hbm, heat_hbm, conc, current,
    conc_in, right_side, pivots,
    heat, staged, slot_rise, current_in, surface_rows, current_rows,
    edges, low_edge, high_edge, faces, base, extra, diagonal, layer_slot, counts, contacts,
    own_sem, heat_send, heat_recv, surf_send, surf_recv, curr_send, curr_recv,
    edge_send, edge_recv, face_send, face_recv,
):
    cell = lax.axis_index("cell")
    sub = lax.axis_index("sub")
    slots, shells, gy, gx = conc_in.shape
    layers, rows, _ = heat.shape[1:]

    offsets = list(range(1, subs))
    far_first = offsets[::-1]

    def at_sub(index):
        return (cell, index)

    first_loads = [
        pltpu.make_async_copy(counts_hbm, counts, own_sem.at[5]),
        pltpu.make_async_copy(heat_hbm, heat, own_sem.at[4]),
        pltpu.make_async_copy(contacts_hbm, contacts, own_sem.at[6]),
    ]
    for load in first_loads:
        load.start()
    barrier = pltpu.get_barrier_semaphore()
    for offset in offsets:
        pl.semaphore_signal(
            barrier, inc=1, device_id=at_sub(peer_of(sub, offset, subs)), device_id_type=MESH
        )
    for offset in range(1, cells):
        pl.semaphore_signal(
            barrier, inc=1, device_id=(peer_of(cell, offset, cells), sub), device_id_type=MESH
        )

    loads = [
        pltpu.make_async_copy(current.at[0], current_in, own_sem.at[0]),
        pltpu.make_async_copy(conc.at[0], conc_in, own_sem.at[1]),
    ]
    for load in loads:
        load.start()

    for load in first_loads:
        load.wait()
    edges[0] = heat[0, :, 0]
    edges[1] = heat[0, :, rows - 1]
    start = jnp.int32(0)
    for index in range(subs):
        held = counts[index]
        for place in range(slots):
            layer = jnp.minimum(start + place, layers - 1)
            staged[index * slots + place] = heat[0, layer]
        start = start + held
    faces[cell] = jnp.zeros((2, rows, gx), jnp.float32)

    def slot_of(layer, carry):
        total = jnp.int32(0)
        slot = layer
        for index in range(subs):
            total = total + counts[index]
            slot = slot + jnp.where(total <= layer, slots - counts[index], 0)
        layer_slot[layer] = jnp.minimum(slot, subs * slots - 1)
        return carry

    pl.semaphore_wait(barrier, subs - 1 + cells - 1)

    sends = []

    def rows_of(index):
        return pl.ds(pl.multiple_of(index * rows, rows), rows)

    def slots_of(index):
        return pl.ds(index * slots, slots)

    def heat_copy(source, target, device):
        return pltpu.make_async_remote_copy(
            src_ref=staged.at[slots_of(target)],
            dst_ref=slot_rise.at[:, rows_of(source)],
            send_sem=heat_send.at[target],
            recv_sem=heat_recv.at[source],
            device_id=at_sub(device),
            device_id_type=MESH,
        )

    def surf_copy(source, target, device):
        return pltpu.make_async_remote_copy(
            src_ref=conc.at[0, :, shells - 1, rows_of(target)],
            dst_ref=surface_rows.at[slots_of(source)],
            send_sem=surf_send.at[target],
            recv_sem=surf_recv.at[source],
            device_id=at_sub(device),
            device_id_type=MESH,
        )

    def curr_copy(source, target, device):
        return pltpu.make_async_remote_copy(
            src_ref=current.at[0, :, rows_of(target)],
            dst_ref=current_rows.at[slots_of(source)],
            send_sem=curr_send.at[target],
            recv_sem=curr_recv.at[source],
            device_id=at_sub(device),
            device_id_type=MESH,
        )

    for offset in far_first:
        other = peer_of(sub, offset, subs)
        copy = heat_copy(sub, other, other)
        copy.start()
        sends.append(copy)

    for offset in far_first:
        other = peer_of(sub, offset, subs)
        for copy in (surf_copy(sub, other, other), curr_copy(sub, other, other)):
            copy.start()
            sends.append(copy)
    to_below = pltpu.make_async_remote_copy(
        src_ref=edges.at[0],
        dst_ref=high_edge,
        send_sem=edge_send.at[0],
        recv_sem=edge_recv.at[0],
        device_id=at_sub(jnp.maximum(sub - 1, 0)),
        device_id_type=MESH,
    )
    to_above = pltpu.make_async_remote_copy(
        src_ref=edges.at[1],
        dst_ref=low_edge,
        send_sem=edge_send.at[1],
        recv_sem=edge_recv.at[1],
        device_id=at_sub(jnp.minimum(sub + 1, subs - 1)),
        device_id_type=MESH,
    )

    @pl.when(sub > 0)
    def _():
        to_below.start()

    @pl.when(sub < subs - 1)
    def _():
        to_above.start()

    def face_copies(source, device):
        return [
            pltpu.make_async_remote_copy(
                src_ref=heat_hbm.at[0, layer],
                dst_ref=faces.at[source, place],
                send_sem=face_send.at[2 * device + place],
                recv_sem=face_recv.at[2 * source + place],
                device_id=(device, sub),
                device_id_type=MESH,
            )
            for place, layer in ((0, 0), (1, layers - 1))
        ]

    for offset in range(1, cells):
        for copy in face_copies(cell, peer_of(cell, offset, cells)):
            copy.start()
            sends.append(copy)

    mine = [
        pltpu.make_async_copy(
            conc.at[0, :, shells - 1, rows_of(sub)], surface_rows.at[slots_of(sub)], own_sem.at[2]
        ),
        pltpu.make_async_copy(
            current.at[0, :, rows_of(sub)], current_rows.at[slots_of(sub)], own_sem.at[3]
        ),
    ]
    for copy in mine:
        copy.start()
    slot_rise[:, rows_of(sub)] = staged[slots_of(sub)]

    lax.fori_loop(0, layers, slot_of, jnp.int32(0))

    live_count = counts[sub]
    live = lax.broadcasted_iota(jnp.int32, (slots, rows, gx), 0) < live_count
    volumes = [((r + 1) ** 3 - r**3) / (3.0 * shells**3) for r in range(shells)]
    weights = [DIFFUSION_STEP * ((r + 1) ** 2 / shells**2 * shells) for r in range(shells - 1)]

    def particle(where):
        rise = slot_rise[:, where]
        speedup = jnp.exp(
            (DIFFUSION_ACTIVATION / BASE_KELVIN) * rise / (BASE_KELVIN + rise)
        )
        uppers = []
        values = []
        link = None
        for r in range(shells):
            right = volumes[r] * conc_in[:, r, where]
            if r == shells - 1:
                right = right - SURFACE_STEP * current_in[:, where]
            pivot = volumes[r]
            if r > 0:
                pivot = pivot + link * (1.0 - uppers[r - 1])
                right = right + link * values[r - 1]
            if r < shells - 1:
                next_link = weights[r] * speedup
                pivot = pivot + next_link
            inverse = 1.0 / pivot
            if r < shells - 1:
                uppers.append(next_link * inverse)
                link = next_link
            values.append(right * inverse)
        result = values[shells - 1]
        conc_in[:, shells - 1, where] = jnp.where(live, result, 0.0)
        for r in range(shells - 2, -1, -1):
            result = values[r] + uppers[r] * result
            conc_in[:, r, where] = jnp.where(live, result, 0.0)

    for load in loads:
        load.wait()
    for offset in [0] + offsets:
        other = peer_of(sub, offset, subs)
        if offset:
            heat_copy(other, sub, other).wait_recv()
        particle(rows_of(other))

    @pl.when(sub > 0)
    def _():
        to_above.wait_recv()

    @pl.when(sub == 0)
    def _():
        low_edge[...] = edges[0]

    @pl.when(sub < subs - 1)
    def _():
        to_below.wait_recv()

    @pl.when(sub == subs - 1)
    def _():
        high_edge[...] = edges[1]

    for offset in range(1, cells):
        other = peer_of(cell, offset, cells)
        for copy in face_copies(other, other):
            copy.wait_recv()

    row_index = lax.broadcasted_iota(jnp.int32, (rows, gx), 0)
    lane_index = lax.broadcasted_iota(jnp.int32, (rows, gx), 1)

    def fill(layer, carry):
        here = heat[0, layer]
        up = pltpu.roll(here, 1, 0)
        up = jnp.where(row_index == 0, low_edge[pl.ds(layer, 1)], up)
        down = pltpu.roll(here, rows - 1, 0)
        down = jnp.where(row_index == rows - 1, high_edge[pl.ds(layer, 1)], down)
        left = jnp.where(lane_index == 0, here, pltpu.roll(here, 1, 1))
        right = jnp.where(lane_index == gx - 1, here, pltpu.roll(here, gx - 1, 1))
        laplace = down + up + right + left - 4.0 * here
        base[layer] = here + INPLANE_CONDUCT * laplace
        return carry

    lax.fori_loop(0, layers, fill, jnp.int32(0), unroll=2)
    lower = contacts[0, cell]
    upper = contacts[1, cell]
    below_face = jnp.where(lower >= 0, faces[jnp.maximum(lower, 0), 1], 0.0)
    above_face = jnp.where(upper >= 0, faces[jnp.maximum(upper, 0), 0], 0.0)
    base[0] = base[0] + CONTACT_CONDUCT * (below_face - heat[0, 0])
    base[layers - 1] = base[layers - 1] + CONTACT_CONDUCT * (above_face - heat[0, layers - 1])

    for offset in [0] + far_first:
        other = peer_of(sub, offset, subs)
        if offset:
            surf_copy(other, sub, other).wait_recv()
            curr_copy(other, sub, other).wait_recv()
        else:
            for copy in mine:
                copy.wait()
        at = slots_of(other)
        rise = staged[at]
        source, slope = kinetics(surface_rows[at], rise, current_rows[at])
        extra[at] = source - slope * rise
        diagonal[at] = 1.0 - slope

    for layer in range(layers):
        slot = layer_slot[layer]
        ends = (layer > 0) + (layer < layers - 1)
        pivots[layer] = diagonal[slot] + ends * THROUGH_CONDUCT
        right_side[layer] = base[layer] + extra[slot]

    for copy in sends:
        copy.wait_send()

    @pl.when(sub > 0)
    def _():
        to_below.wait_send()

    @pl.when(sub < subs - 1)
    def _():
        to_above.wait_send()


def finish(conc, right_side, pivots, conc_new, heat_new, sem):
    slots = conc.shape[0]
    layers = right_side.shape[0]
    writes = [
        pltpu.make_async_copy(conc.at[s], conc_new.at[0, s], sem.at[s]) for s in range(slots)
    ]
    for write in writes:
        write.start()

    def sweep(order):
        factors, values = [], []
        for layer in order:
            pivot, right = pivots[layer], right_side[layer]
            if factors:
                pivot = pivot - THROUGH_CONDUCT * factors[-1]
                right = right + THROUGH_CONDUCT * values[-1]
            inverse = 1.0 / pivot
            factors.append(THROUGH_CONDUCT * inverse)
            values.append(right * inverse)
        return factors, values

    middle = layers // 2
    low_f, low_v = sweep(range(middle))
    high_f, high_v = sweep(range(layers - 1, middle - 1, -1))
    low = (low_v[-1] + low_f[-1] * high_v[-1]) / (1.0 - low_f[-1] * high_f[-1])
    high = high_v[-1] + high_f[-1] * low
    heat_new[0, middle - 1] = low
    heat_new[0, middle] = high
    for step in range(middle - 2, -1, -1):
        low = low_v[step] + low_f[step] * low
        heat_new[0, step] = low
    for step in range(len(high_v) - 2, -1, -1):
        high = high_v[step] + high_f[step] * high
        heat_new[0, layers - 1 - step] = high
    for write in writes:
        write.wait()


def per_device(cells, subs, shell_conc, heat_rise, layer_current, layer_counts, contacts):
    _, slots, shells, gy, gx = shell_conc.shape
    _, layers, rows, _ = heat_rise.shape
    f32 = jnp.float32
    dma = pltpu.SemaphoreType.DMA
    table = (layers, rows, gx)
    held = [
        pltpu.with_memory_space_constraint(array, pltpu.HBM)
        for array in (layer_counts, contacts.T, heat_rise, shell_conc, layer_current)
    ]
    conc, right_side, pivots = pl.pallas_call(
        functools.partial(kernel, cells, subs),
        out_shape=(
            pltpu.VMEM((slots, shells, gy, gx), f32),
            pltpu.VMEM(table, f32),
            pltpu.VMEM(table, f32),
        ),
        in_specs=[
            pl.BlockSpec(memory_space=pltpu.HBM)
        ] * 5,
        out_specs=(pl.BlockSpec(memory_space=pltpu.VMEM),) * 3,
        scratch_shapes=[
            pltpu.VMEM(heat_rise.shape, f32),
            pltpu.VMEM((subs * slots, rows, gx), f32),
            pltpu.VMEM((slots, gy, gx), f32),
            pltpu.VMEM((slots, gy, gx), f32),
            pltpu.VMEM((subs * slots, rows, gx), f32),
            pltpu.VMEM((subs * slots, rows, gx), f32),
            pltpu.VMEM((2, layers, gx), f32),
            pltpu.VMEM((layers, gx), f32),
            pltpu.VMEM((layers, gx), f32),
            pltpu.VMEM((cells, 2, rows, gx), f32),
            pltpu.VMEM(table, f32),
            pltpu.VMEM((subs * slots, rows, gx), f32),
            pltpu.VMEM((subs * slots, rows, gx), f32),
            pltpu.SMEM((layers,), jnp.int32),
            pltpu.SMEM(layer_counts.shape, jnp.int32),
            pltpu.SMEM(contacts.shape[::-1], jnp.int32),
            dma((7,)),
            dma((subs,)),
            dma((subs,)),
            dma((subs,)),
            dma((subs,)),
            dma((subs,)),
            dma((subs,)),
            dma((2,)),
            dma((2,)),
            dma((2 * cells,)),
            dma((2 * cells,)),
        ],
        compiler_params=pltpu.CompilerParams(
            collective_id=0, has_side_effects=True, vmem_limit_bytes=GRANT
        ),
    )(*held)
    conc_new, heat_new = pl.pallas_call(
        finish,
        out_shape=(
            jax.ShapeDtypeStruct(shell_conc.shape, f32),
            jax.ShapeDtypeStruct(heat_rise.shape, f32),
        ),
        in_specs=[pl.BlockSpec(memory_space=pltpu.VMEM)] * 3,
        out_specs=(
            pl.BlockSpec(memory_space=pl.ANY),
            pl.BlockSpec(memory_space=pltpu.VMEM),
        ),
        scratch_shapes=[dma((slots,))],
        compiler_params=pltpu.CompilerParams(vmem_limit_bytes=GRANT),
    )(conc, right_side, pivots)
    return conc_new, heat_new


def solution(mesh):
    in_specs = (
        P("cell", "sub", None, None, None),
        P("cell", None, "sub", None),
        P("cell", "sub", None, None),
        P(),
        P(),
    )
    out_specs = (P("cell", "sub", None, None, None), P("cell", None, "sub", None))
    body = functools.partial(per_device, mesh.shape["cell"], mesh.shape["sub"])
    return jax.shard_map(
        body, mesh=mesh, in_specs=in_specs, out_specs=out_specs, check_vma=False
    )
```

profile of v0, /device:TPU:0, one launch (start us, length us, event | category | flops | bytes accessed | tf_op | source)
XLA Modules:
  0.0 27.9 jit_solution(7546387524181654005)
XLA Ops:
  0.6 25.0 %shard_map.68 = (f32[4,10,128,128]{3,2,1,0:T(8,128)S(1)}, f32[30,16,128]{2,1,0:T(8,128)S(1)}, f32[30,16,128]{2,1,0:T(8,128)S(1)}) custom-call(s32[8]{0:T(128)} %counts_hbm.1, s32[2,4]{1,0:T(2,128)} %bitcast.1, f32[1,30,16,128]{3,2,1,0:T(8,128)} %heat_hbm.1, f32[1,4,10,128,128]{4,3,2,1,0:T(8,128)} %conc.1, f32[1,4,128,128]{3,2,1,0:T(8,128)} %current.1), custom_call_target="tpu_custom_call" | custom-call | tf_op jit(solution)/shard_map/pallas_call | solution.py:411
  25.7 2.2 %shard_map.69 = (f32[1,4,10,128,128]{4,3,2,1,0:T(8,128)}, f32[1,30,16,128]{3,2,1,0:T(8,128)}) custom-call(f32[4,10,128,128]{3,2,1,0:T(8,128)S(1)} %get-tuple-element.5.conc, f32[30,16,128]{2,1,0:T(8,128)S(1)} %get-tuple-element.6.right_side, f32[30,16,128]{2,1,0:T(8,128)S(1)} %get-tuple-element.7.pivots), custom_call_target="tpu_custom_call" | custom-call | tf_op jit(solution)/shard_map/pallas_call | solution.py:455
where the time goes:
time: 28 us; the launch traced here: 27.9 us
  Pallas kernels  27.2 us (97%)
  between operations  0.64 us (2%)
    pallas_call x1, Pallas kernels, per_device(): pl.pallas_call(functools.partial(kernel, cells, subs), out_shape=(pltpu.V...  25 us
    pallas_call x1, Pallas kernels, per_device(): pl.pallas_call(finish, out_shape=(jax.ShapeDtypeStruct(shell_conc.shape,...  2.21 us

commit v1 on v0

--- a/solution.py
+++ b/solution.py
@@ -21,6 +21,7 @@
 CONTACT_CONDUCT = 0.5
 MESH = pl.DeviceIdType.MESH
 GRANT = 24 << 20
+PAIR = 2
 
 
 def partner(me, offset):
@@ -31,12 +32,6 @@
             result = result + bit * (1 - 2 * ((me // bit) % 2))
         bit *= 2
     return result
-
-
-def peer_of(me, offset, count):
-    if count & (count - 1) == 0:
-        return partner(me, offset)
-    return (me + offset) % count
 
 
 def inverse_sine(value):
@@ -73,7 +68,7 @@
     conc_in, right_side, pivots,
     heat, staged, slot_rise, current_in, surface_rows, current_rows,
     edges, low_edge, high_edge, faces, base, extra, diagonal, layer_slot, counts, contacts,
-    own_sem, heat_send, heat_recv, surf_send, surf_recv, curr_send, curr_recv,
+    reach, cell_reach, own_sem, heat_send, heat_recv, surf_send, surf_recv, curr_send, curr_recv,
     edge_send, edge_recv, face_send, face_recv,
 ):
     cell = lax.axis_index("cell")
@@ -82,7 +77,15 @@
     layers, rows, _ = heat.shape[1:]
 
     offsets = list(range(1, subs))
-    far_first = offsets[::-1]
+    arrivals = offsets[: PAIR - 1] + offsets[2 * PAIR - 2 : PAIR - 2 : -1] + offsets[: 2 * PAIR - 2 : -1]
+    chip, core, chips = sub // PAIR, sub % PAIR, subs // PAIR
+    cell_bits = [1 << bit for bit in range(cells.bit_length() - 1)]
+
+    def has_chip(shift):
+        return jnp.logical_and(chip + shift >= 0, chip + shift < chips)
+
+    def on_chip(shift, place):
+        return jnp.clip(chip + shift, 0, chips - 1) * PAIR + place
 
     def at_sub(index):
         return (cell, index)
@@ -95,14 +98,21 @@
     for load in first_loads:
         load.start()
     barrier = pltpu.get_barrier_semaphore()
-    for offset in offsets:
-        pl.semaphore_signal(
-            barrier, inc=1, device_id=at_sub(peer_of(sub, offset, subs)), device_id_type=MESH
-        )
-    for offset in range(1, cells):
-        pl.semaphore_signal(
-            barrier, inc=1, device_id=(peer_of(cell, offset, cells), sub), device_id_type=MESH
-        )
+
+    def greet(device):
+        pl.semaphore_signal(barrier, inc=1, device_id=device, device_id_type=MESH)
+
+    for place in range(1, PAIR):
+        greet(at_sub(chip * PAIR + (core + place) % PAIR))
+    for shift in (-1, 1):
+
+        @pl.when(has_chip(shift))
+        def _():
+            for place in range(PAIR):
+                greet(at_sub(on_chip(shift, place)))
+
+    for bit in cell_bits:
+        greet((partner(cell, bit), sub))
 
     loads = [
         pltpu.make_async_copy(current.at[0], current_in, own_sem.at[0]),
@@ -111,6 +121,89 @@
     for load in loads:
         load.start()
 
+    beside = has_chip(-1).astype(jnp.int32) + has_chip(1).astype(jnp.int32)
+    pl.semaphore_wait(barrier, PAIR - 1 + PAIR * beside + len(cell_bits))
+
+    def relay(distance):
+        for way, shift in enumerate((1, -1)):
+
+            @pl.when(jnp.logical_and(has_chip(-shift), has_chip(shift * (distance - 1))))
+            def _():
+                pl.semaphore_signal(
+                    reach.at[way, distance - 1],
+                    inc=1,
+                    device_id=at_sub(on_chip(-shift, core)),
+                    device_id_type=MESH,
+                )
+
+    def learn(distance):
+        for way, shift in enumerate((1, -1)):
+
+            @pl.when(has_chip(shift * distance))
+            def _():
+                pl.semaphore_wait(reach.at[way, distance - 1], 1)
+
+    if chips > 2:
+        relay(2)
+    for stage, bit in enumerate(cell_bits[:-1]):
+        pl.semaphore_signal(
+            cell_reach.at[stage], inc=1, device_id=(partner(cell, bit), sub), device_id_type=MESH
+        )
+        if stage + 1 < len(cell_bits) - 1:
+            pl.semaphore_wait(cell_reach.at[stage], 1)
+
+    sends = []
+
+    def rows_of(index):
+        return pl.ds(pl.multiple_of(index * rows, rows), rows)
+
+    def slots_of(index):
+        return pl.ds(index * slots, slots)
+
+    def heat_copy(source, target, device):
+        return pltpu.make_async_remote_copy(
+            src_ref=staged.at[slots_of(target)],
+            dst_ref=slot_rise.at[:, rows_of(source)],
+            send_sem=heat_send.at[target],
+            recv_sem=heat_recv.at[source],
+            device_id=at_sub(device),
+            device_id_type=MESH,
+        )
+
+    def surf_copy(source, target, device):
+        return pltpu.make_async_remote_copy(
+            src_ref=conc.at[0, :, shells - 1, rows_of(target)],
+            dst_ref=surface_rows.at[slots_of(source)],
+            send_sem=surf_send.at[target],
+            recv_sem=surf_recv.at[source],
+            device_id=at_sub(device),
+            device_id_type=MESH,
+        )
+
+    def curr_copy(source, target, device):
+        return pltpu.make_async_remote_copy(
+            src_ref=current.at[0, :, rows_of(target)],
+            dst_ref=current_rows.at[slots_of(source)],
+            send_sem=curr_send.at[target],
+            recv_sem=curr_recv.at[source],
+            device_id=at_sub(device),
+            device_id_type=MESH,
+        )
+
+    inner = jnp.logical_and(has_chip(-1), has_chip(1))
+    outer = jnp.logical_not(inner)
+
+    def issue(distance, makers, when=True):
+        for shift in (distance, -distance) if distance else (0,):
+
+            @pl.when(jnp.logical_and(has_chip(shift), when))
+            def _():
+                for make in makers:
+                    for place in range(PAIR) if distance else range(1, PAIR):
+                        other = on_chip(shift, place if distance else (core + place) % PAIR)
+                        make(sub, other, other).start()
+
+    issue(1, (surf_copy, curr_copy), outer)
     for load in first_loads:
         load.wait()
     edges[0] = heat[0, :, 0]
@@ -124,66 +217,8 @@
         start = start + held
     faces[cell] = jnp.zeros((2, rows, gx), jnp.float32)
 
-    def slot_of(layer, carry):
-        total = jnp.int32(0)
-        slot = layer
-        for index in range(subs):
-            total = total + counts[index]
-            slot = slot + jnp.where(total <= layer, slots - counts[index], 0)
-        layer_slot[layer] = jnp.minimum(slot, subs * slots - 1)
-        return carry
-
-    pl.semaphore_wait(barrier, subs - 1 + cells - 1)
-
-    sends = []
-
-    def rows_of(index):
-        return pl.ds(pl.multiple_of(index * rows, rows), rows)
-
-    def slots_of(index):
-        return pl.ds(index * slots, slots)
-
-    def heat_copy(source, target, device):
-        return pltpu.make_async_remote_copy(
-            src_ref=staged.at[slots_of(target)],
-            dst_ref=slot_rise.at[:, rows_of(source)],
-            send_sem=heat_send.at[target],
-            recv_sem=heat_recv.at[source],
-            device_id=at_sub(device),
-            device_id_type=MESH,
-        )
-
-    def surf_copy(source, target, device):
-        return pltpu.make_async_remote_copy(
-            src_ref=conc.at[0, :, shells - 1, rows_of(target)],
-            dst_ref=surface_rows.at[slots_of(source)],
-            send_sem=surf_send.at[target],
-            recv_sem=surf_recv.at[source],
-            device_id=at_sub(device),
-            device_id_type=MESH,
-        )
-
-    def curr_copy(source, target, device):
-        return pltpu.make_async_remote_copy(
-            src_ref=current.at[0, :, rows_of(target)],
-            dst_ref=current_rows.at[slots_of(source)],
-            send_sem=curr_send.at[target],
-            recv_sem=curr_recv.at[source],
-            device_id=at_sub(device),
-            device_id_type=MESH,
-        )
-
-    for offset in far_first:
-        other = peer_of(sub, offset, subs)
-        copy = heat_copy(sub, other, other)
-        copy.start()
-        sends.append(copy)
-
-    for offset in far_first:
-        other = peer_of(sub, offset, subs)
-        for copy in (surf_copy(sub, other, other), curr_copy(sub, other, other)):
-            copy.start()
-            sends.append(copy)
+    issue(1, (heat_copy,))
+    issue(0, (heat_copy, surf_copy, curr_copy))
     to_below = pltpu.make_async_remote_copy(
         src_ref=edges.at[0],
         dst_ref=high_edge,
@@ -209,6 +244,18 @@
     def _():
         to_above.start()
 
+    far = range(chips - 1, 1, -1)
+    for distance in range(2, chips):
+        learn(distance)
+        if distance + 1 < chips:
+            relay(distance + 1)
+    for distance in far:
+        issue(distance, (heat_copy,))
+    for distance in far:
+        issue(distance, (surf_copy, curr_copy))
+
+    issue(1, (surf_copy, curr_copy,), inner)
+
     def face_copies(source, device):
         return [
             pltpu.make_async_remote_copy(
@@ -222,8 +269,10 @@
             for place, layer in ((0, 0), (1, layers - 1))
         ]
 
+    if len(cell_bits) > 1:
+        pl.semaphore_wait(cell_reach.at[len(cell_bits) - 2], 1)
     for offset in range(1, cells):
-        for copy in face_copies(cell, peer_of(cell, offset, cells)):
+        for copy in face_copies(cell, partner(cell, offset)):
             copy.start()
             sends.append(copy)
 
@@ -238,6 +287,15 @@
     for copy in mine:
         copy.start()
     slot_rise[:, rows_of(sub)] = staged[slots_of(sub)]
+
+    def slot_of(layer, carry):
+        total = jnp.int32(0)
+        slot = layer
+        for index in range(subs):
+            total = total + counts[index]
+            slot = slot + jnp.where(total <= layer, slots - counts[index], 0)
+        layer_slot[layer] = jnp.minimum(slot, subs * slots - 1)
+        return carry
 
     lax.fori_loop(0, layers, slot_of, jnp.int32(0))
 
@@ -278,8 +336,8 @@
 
     for load in loads:
         load.wait()
-    for offset in [0] + offsets:
-        other = peer_of(sub, offset, subs)
+    for offset in [0] + arrivals:
+        other = partner(sub, offset)
         if offset:
             heat_copy(other, sub, other).wait_recv()
         particle(rows_of(other))
@@ -301,7 +359,7 @@
         high_edge[...] = edges[1]
 
     for offset in range(1, cells):
-        other = peer_of(cell, offset, cells)
+        other = partner(cell, offset)
         for copy in face_copies(other, other):
             copy.wait_recv()
 
@@ -328,8 +386,8 @@
     base[0] = base[0] + CONTACT_CONDUCT * (below_face - heat[0, 0])
     base[layers - 1] = base[layers - 1] + CONTACT_CONDUCT * (above_face - heat[0, layers - 1])
 
-    for offset in [0] + far_first:
-        other = peer_of(sub, offset, subs)
+    for offset in [0] + arrivals:
+        other = partner(sub, offset)
         if offset:
             surf_copy(other, sub, other).wait_recv()
             curr_copy(other, sub, other).wait_recv()
@@ -348,6 +406,10 @@
         pivots[layer] = diagonal[slot] + ends * THROUGH_CONDUCT
         right_side[layer] = base[layer] + extra[slot]
 
+    for offset in offsets:
+        other = partner(sub, offset)
+        for make in (heat_copy, surf_copy, curr_copy):
+            make(sub, other, other).wait_send()
     for copy in sends:
         copy.wait_send()
 
@@ -360,7 +422,7 @@
         to_above.wait_send()
 
 
-def finish(conc, right_side, pivots, conc_new, heat_new, sem):
+def finish(conc, right_side, pivots, conc_new, heat_out, heat_new, sem):
     slots = conc.shape[0]
     layers = right_side.shape[0]
     writes = [
@@ -394,8 +456,11 @@
     for step in range(len(high_v) - 2, -1, -1):
         high = high_v[step] + high_f[step] * high
         heat_new[0, layers - 1 - step] = high
+    heat_write = pltpu.make_async_copy(heat_new, heat_out, sem.at[slots])
+    heat_write.start()
     for write in writes:
         write.wait()
+    heat_write.wait()
 
 
 def per_device(cells, subs, shell_conc, heat_rise, layer_current, layer_counts, contacts):
@@ -436,6 +501,8 @@
             pltpu.SMEM((layers,), jnp.int32),
             pltpu.SMEM(layer_counts.shape, jnp.int32),
             pltpu.SMEM(contacts.shape[::-1], jnp.int32),
+            pltpu.SemaphoreType.REGULAR((2, max(subs // PAIR, 2))),
+            pltpu.SemaphoreType.REGULAR((max(cells.bit_length() - 2, 1),)),
             dma((7,)),
             dma((subs,)),
             dma((subs,)),
@@ -461,9 +528,9 @@
         in_specs=[pl.BlockSpec(memory_space=pltpu.VMEM)] * 3,
         out_specs=(
             pl.BlockSpec(memory_space=pl.ANY),
-            pl.BlockSpec(memory_space=pltpu.VMEM),
+            pl.BlockSpec(memory_space=pl.ANY),
         ),
-        scratch_shapes=[dma((slots,))],
+        scratch_shapes=[pltpu.VMEM(heat_rise.shape, f32), dma((slots + 1,))],
         compiler_params=pltpu.CompilerParams(vmem_limit_bytes=GRANT),
     )(conc, right_side, pivots)
     return conc_new, heat_new

time: 28 us -> 24.9 us (0.89)
  the two profiles are of different devices: /device:TPU:0 before, /device:TPU:9 now
where the time goes in v1:
time: 24.9 us; the launch traced here: 24.7 us
  Pallas kernels  24.1 us (97%)
  between operations  0.64 us (3%)
    pallas_call x1, Pallas kernels, per_device(): pl.pallas_call(functools.partial(kernel, cells, subs), out_shape=(pltpu.V...  22.5 us
    pallas_call x1, Pallas kernels, per_device(): pl.pallas_call(finish, out_shape=(jax.ShapeDtypeStruct(shell_conc.shape,...  1.6 us

profile of v1, /device:TPU:9, one launch (start us, length us, event | category | flops | bytes accessed | tf_op | source)
XLA Modules:
  0.0 24.7 jit_solution(14717836429764343982)
XLA Ops:
  0.6 22.5 %shard_map.68 = (f32[4,10,128,128]{3,2,1,0:T(8,128)S(1)}, f32[30,16,128]{2,1,0:T(8,128)S(1)}, f32[30,16,128]{2,1,0:T(8,128)S(1)}) custom-call(s32[8]{0:T(128)} %counts_hbm.1, s32[2,4]{1,0:T(2,128)} %bitcast.1, f32[1,30,16,128]{3,2,1,0:T(8,128)} %heat_hbm.1, f32[1,4,10,128,128]{4,3,2,1,0:T(8,128)} %conc.1, f32[1,4,128,128]{3,2,1,0:T(8,128)} %current.1), custom_call_target="tpu_custom_call" | custom-call | tf_op jit(solution)/shard_map/pallas_call | solution.py:476
  23.1 1.6 %shard_map.69 = (f32[1,4,10,128,128]{4,3,2,1,0:T(8,128)}, f32[1,30,16,128]{3,2,1,0:T(8,128)}) custom-call(f32[4,10,128,128]{3,2,1,0:T(8,128)S(1)} %get-tuple-element.5.conc, f32[30,16,128]{2,1,0:T(8,128)S(1)} %get-tuple-element.6.right_side, f32[30,16,128]{2,1,0:T(8,128)S(1)} %get-tuple-element.7.pivots), custom_call_target="tpu_custom_call" | custom-call | tf_op jit(solution)/shard_map/pallas_call | solution.py:522

commit v2 on v1

--- a/solution.py
+++ b/solution.py
@@ -104,15 +104,20 @@
 
     for place in range(1, PAIR):
         greet(at_sub(chip * PAIR + (core + place) % PAIR))
+    inward = jnp.where(2 * chip < chips, 1, -1)
+    middle = jnp.logical_or(chip == chips // 2 - 1, chip == chips // 2)
     for shift in (-1, 1):
 
-        @pl.when(has_chip(shift))
+        @pl.when(jnp.logical_and(has_chip(shift), jnp.logical_or(inward != shift, middle)))
         def _():
             for place in range(PAIR):
                 greet(at_sub(on_chip(shift, place)))
 
     for bit in cell_bits:
-        greet((partner(cell, bit), sub))
+
+        @pl.when((cell // bit) % 2 == 0)
+        def _():
+            greet((partner(cell, bit), sub))
 
     loads = [
         pltpu.make_async_copy(current.at[0], current_in, own_sem.at[0]),
@@ -121,36 +126,41 @@
     for load in loads:
         load.start()
 
-    beside = has_chip(-1).astype(jnp.int32) + has_chip(1).astype(jnp.int32)
-    pl.semaphore_wait(barrier, PAIR - 1 + PAIR * beside + len(cell_bits))
+    lower = sum((cell // bit) % 2 for bit in cell_bits)
+    pl.semaphore_wait(barrier, PAIR - 1 + (PAIR if chips > 1 else 0) + lower)
+
+    def tell(semaphore, device):
+        pl.semaphore_signal(semaphore, inc=1, device_id=device, device_id_type=MESH)
+
+    for way, shift in enumerate((1, -1)):
+
+        @pl.when(jnp.logical_and(inward == -shift, jnp.logical_not(middle)))
+        def _():
+            tell(reach.at[way, 0], at_sub(on_chip(-shift, core)))
+
+    for place, bit in enumerate(cell_bits):
+
+        @pl.when((cell // bit) % 2 == 1)
+        def _():
+            tell(cell_reach.at[0, place], (partner(cell, bit), sub))
 
     def relay(distance):
         for way, shift in enumerate((1, -1)):
 
             @pl.when(jnp.logical_and(has_chip(-shift), has_chip(shift * (distance - 1))))
             def _():
-                pl.semaphore_signal(
-                    reach.at[way, distance - 1],
-                    inc=1,
-                    device_id=at_sub(on_chip(-shift, core)),
-                    device_id_type=MESH,
-                )
+                tell(reach.at[way, distance - 1], at_sub(on_chip(-shift, core)))
 
     def learn(distance):
         for way, shift in enumerate((1, -1)):
 
-            @pl.when(has_chip(shift * distance))
+            known = has_chip(shift * distance)
+            if distance == 1:
+                known = jnp.logical_and(known, inward != shift)
+
+            @pl.when(known)
             def _():
                 pl.semaphore_wait(reach.at[way, distance - 1], 1)
-
-    if chips > 2:
-        relay(2)
-    for stage, bit in enumerate(cell_bits[:-1]):
-        pl.semaphore_signal(
-            cell_reach.at[stage], inc=1, device_id=(partner(cell, bit), sub), device_id_type=MESH
-        )
-        if stage + 1 < len(cell_bits) - 1:
-            pl.semaphore_wait(cell_reach.at[stage], 1)
 
     sends = []
 
@@ -193,10 +203,14 @@
     inner = jnp.logical_and(has_chip(-1), has_chip(1))
     outer = jnp.logical_not(inner)
 
-    def issue(distance, makers, when=True):
+    def issue(distance, makers, when=True, within=None):
         for shift in (distance, -distance) if distance else (0,):
 
-            @pl.when(jnp.logical_and(has_chip(shift), when))
+            wanted = jnp.logical_and(has_chip(shift), when)
+            if within is not None:
+                wanted = jnp.logical_and(wanted, (inward == shift) == within)
+
+            @pl.when(wanted)
             def _():
                 for make in makers:
                     for place in range(PAIR) if distance else range(1, PAIR):
@@ -217,7 +231,11 @@
         start = start + held
     faces[cell] = jnp.zeros((2, rows, gx), jnp.float32)
 
-    issue(1, (heat_copy,))
+    issue(1, (heat_copy,), within=True)
+    learn(1)
+    if chips > 2:
+        relay(2)
+    issue(1, (heat_copy,), within=False)
     issue(0, (heat_copy, surf_copy, curr_copy))
     to_below = pltpu.make_async_remote_copy(
         src_ref=edges.at[0],
@@ -250,11 +268,7 @@
         if distance + 1 < chips:
             relay(distance + 1)
     for distance in far:
-        issue(distance, (heat_copy,))
-    for distance in far:
-        issue(distance, (surf_copy, curr_copy))
-
-    issue(1, (surf_copy, curr_copy,), inner)
+        issue(distance, (heat_copy, surf_copy, curr_copy))
 
     def face_copies(source, device):
         return [
@@ -269,12 +283,28 @@
             for place, layer in ((0, 0), (1, layers - 1))
         ]
 
+    for place, bit in enumerate(cell_bits):
+
+        @pl.when((cell // bit) % 2 == 0)
+        def _():
+            pl.semaphore_wait(cell_reach.at[0, place], 1)
+
+    def spread(place):
+        tell(cell_reach.at[1, place], (partner(cell, cell_bits[place]), sub))
+
     if len(cell_bits) > 1:
-        pl.semaphore_wait(cell_reach.at[len(cell_bits) - 2], 1)
-    for offset in range(1, cells):
-        for copy in face_copies(cell, partner(cell, offset)):
-            copy.start()
-            sends.append(copy)
+        spread(0)
+
+    def send_faces():
+        for place in range(len(cell_bits) - 1):
+            pl.semaphore_wait(cell_reach.at[1, place], 1)
+            if place + 1 < len(cell_bits) - 1:
+                spread(place + 1)
+        for offset in range(1, cells):
+            for copy in face_copies(cell, partner(cell, offset)):
+                copy.start()
+                sends.append(copy)
+
 
     mine = [
         pltpu.make_async_copy(
@@ -336,11 +366,17 @@
 
     for load in loads:
         load.wait()
-    for offset in [0] + arrivals:
+    for count, offset in enumerate([0] + arrivals):
         other = partner(sub, offset)
         if offset:
             heat_copy(other, sub, other).wait_recv()
+        if count == 4:
+            issue(1, (surf_copy, curr_copy), inner, True)
+        if count == 2:
+            issue(1, (surf_copy, curr_copy), inner, False)
         particle(rows_of(other))
+        if count == 0:
+            send_faces()
 
     @pl.when(sub > 0)
     def _():
@@ -502,7 +538,7 @@
             pltpu.SMEM(layer_counts.shape, jnp.int32),
             pltpu.SMEM(contacts.shape[::-1], jnp.int32),
             pltpu.SemaphoreType.REGULAR((2, max(subs // PAIR, 2))),
-            pltpu.SemaphoreType.REGULAR((max(cells.bit_length() - 2, 1),)),
+            pltpu.SemaphoreType.REGULAR((2, max(cells.bit_length() - 1, 1))),
             dma((7,)),
             dma((subs,)),
             dma((subs,)),

time: 24.9 us -> 24.1 us (0.968)
  Pallas kernels: 24.1 us -> 23.3 us
    pallas_call x1, Pallas kernels: 22.5 us -> 21.7 us  [per_device(): pl.pallas_call(functools.partial(kernel, cells, subs), out_shape=(pltpu.V...]
where the time goes in v2:
time: 24.1 us; the launch traced here: 23.9 us
  Pallas kernels  23.3 us (97%)
  between operations  0.64 us (3%)
    pallas_call x1, Pallas kernels, per_device(): pl.pallas_call(functools.partial(kernel, cells, subs), out_shape=(pltpu.V...  21.7 us
    pallas_call x1, Pallas kernels, per_device(): pl.pallas_call(finish, out_shape=(jax.ShapeDtypeStruct(shell_conc.shape,...  1.6 us

profile of v2, /device:TPU:9, one launch (start us, length us, event | category | flops | bytes accessed | tf_op | source)
XLA Modules:
  0.0 23.9 jit_solution(16566291973340146574)
XLA Ops:
  0.6 21.7 %shard_map.68 = (f32[4,10,128,128]{3,2,1,0:T(8,128)S(1)}, f32[30,16,128]{2,1,0:T(8,128)S(1)}, f32[30,16,128]{2,1,0:T(8,128)S(1)}) custom-call(s32[8]{0:T(128)} %counts_hbm.1, s32[2,4]{1,0:T(2,128)} %bitcast.1, f32[1,30,16,128]{3,2,1,0:T(8,128)} %heat_hbm.1, f32[1,4,10,128,128]{4,3,2,1,0:T(8,128)} %conc.1, f32[1,4,128,128]{3,2,1,0:T(8,128)} %current.1), custom_call_target="tpu_custom_call" | custom-call | tf_op jit(solution)/shard_map/pallas_call | solution.py:512
  22.3 1.6 %shard_map.69 = (f32[1,4,10,128,128]{4,3,2,1,0:T(8,128)}, f32[1,30,16,128]{3,2,1,0:T(8,128)}) custom-call(f32[4,10,128,128]{3,2,1,0:T(8,128)S(1)} %get-tuple-element.5.conc, f32[30,16,128]{2,1,0:T(8,128)S(1)} %get-tuple-element.6.right_side, f32[30,16,128]{2,1,0:T(8,128)S(1)} %get-tuple-element.7.pivots), custom_call_target="tpu_custom_call" | custom-call | tf_op jit(solution)/shard_map/pallas_call | solution.py:558

commit v3 on v2

--- a/solution.py
+++ b/solution.py
@@ -65,11 +65,13 @@
 def kernel(
     cells, subs,
     counts_hbm, contacts_hbm, heat_hbm, conc, current,
-    conc_in, right_side, pivots,
+    conc_in, answer,
     heat, staged, slot_rise, current_in, surface_rows, current_rows,
-    edges, low_edge, high_edge, faces, base, extra, diagonal, layer_slot, counts, contacts,
+    edges, low_edge, high_edge, faces, base, extra, diagonal, layer_slot, slot_layer, counts, contacts,
+    twin_out, twin_in, solved, factors, values, contact_out, contact_in, match_out, match_in, part, border_out, border_in,
     reach, cell_reach, own_sem, heat_send, heat_recv, surf_send, surf_recv, curr_send, curr_recv,
     edge_send, edge_recv, face_send, face_recv,
+    twin_send, twin_recv, pair_send, pair_recv, border_send, border_recv,
 ):
     cell = lax.axis_index("cell")
     sub = lax.axis_index("sub")
@@ -80,6 +82,15 @@
     arrivals = offsets[: PAIR - 1] + offsets[2 * PAIR - 2 : PAIR - 2 : -1] + offsets[: 2 * PAIR - 2 : -1]
     chip, core, chips = sub // PAIR, sub % PAIR, subs // PAIR
     cell_bits = [1 << bit for bit in range(cells.bit_length() - 1)]
+
+    half = subs // 2
+    own_slots = half * slots
+    left = 2 * chip < chips
+    ours = jnp.where(left, chips // 2 - 1, chips // 2)
+    theirs = chips - 1 - ours
+    own_first = jnp.where(left, 0, own_slots)
+    other_first = own_slots - own_first
+    twin = theirs * PAIR + core
 
     def has_chip(shift):
         return jnp.logical_and(chip + shift >= 0, chip + shift < chips)
@@ -207,6 +218,9 @@
         for shift in (distance, -distance) if distance else (0,):
 
             wanted = jnp.logical_and(has_chip(shift), when)
+            if distance and heat_copy not in makers:
+                crossing = jnp.logical_and(chip + shift == theirs, distance > 0)
+                wanted = jnp.logical_and(wanted, jnp.logical_not(crossing))
             if within is not None:
                 wanted = jnp.logical_and(wanted, (inward == shift) == within)
 
@@ -217,7 +231,7 @@
                         other = on_chip(shift, place if distance else (core + place) % PAIR)
                         make(sub, other, other).start()
 
-    issue(1, (surf_copy, curr_copy), outer)
+    issue(1, (curr_copy, surf_copy), outer)
     for load in first_loads:
         load.wait()
     edges[0] = heat[0, :, 0]
@@ -228,6 +242,8 @@
         for place in range(slots):
             layer = jnp.minimum(start + place, layers - 1)
             staged[index * slots + place] = heat[0, layer]
+            slot_layer[index * slots + place] = layer
+            border_out[index, place] = heat[0, layer, jnp.where(left, rows - 1, 0)]
         start = start + held
     faces[cell] = jnp.zeros((2, rows, gx), jnp.float32)
 
@@ -267,8 +283,33 @@
         learn(distance)
         if distance + 1 < chips:
             relay(distance + 1)
+    bordering = jnp.logical_and(
+        chip == ours + jnp.where(left, -1, 1), core == jnp.where(left, PAIR - 1, 0)
+    )
+
+    def border_copy(target):
+        return pltpu.make_async_remote_copy(
+            src_ref=border_out.at[target],
+            dst_ref=border_in,
+            send_sem=border_send.at[target],
+            recv_sem=border_recv.at[0],
+            device_id=at_sub(target),
+            device_id_type=MESH,
+        )
+
+    def borders(act):
+        @pl.when(bordering)
+        def _():
+            for place in range(half):
+                act(border_copy(jnp.where(left, half + place, place)))
+
+    borders(lambda copy: copy.start())
     for distance in far:
-        issue(distance, (heat_copy, surf_copy, curr_copy))
+        issue(distance, (heat_copy,))
+    for distance in far:
+        issue(distance, (surf_copy, curr_copy), inner)
+    for distance in far:
+        issue(distance, (surf_copy,), jnp.logical_and(outer, left))
 
     def face_copies(source, device):
         return [
@@ -366,17 +407,77 @@
 
     for load in loads:
         load.wait()
-    for count, offset in enumerate([0] + arrivals):
+    near = [0] + arrivals[: 2 * PAIR - 1]
+    rest = arrivals[2 * PAIR - 1 :]
+    for count, offset in enumerate(near):
         other = partner(sub, offset)
         if offset:
             heat_copy(other, sub, other).wait_recv()
-        if count == 4:
-            issue(1, (surf_copy, curr_copy), inner, True)
-        if count == 2:
-            issue(1, (surf_copy, curr_copy), inner, False)
         particle(rows_of(other))
         if count == 0:
             send_faces()
+        if count == 1:
+            issue(1, (surf_copy, curr_copy), inner)
+    row_index = lax.broadcasted_iota(jnp.int32, (rows, gx), 0)
+    lane_index = lax.broadcasted_iota(jnp.int32, (rows, gx), 1)
+
+    def smoothed(here, before, after):
+        up = jnp.where(row_index == 0, before, pltpu.roll(here, 1, 0))
+        down = jnp.where(row_index == rows - 1, after, pltpu.roll(here, rows - 1, 0))
+        left_side = jnp.where(lane_index == 0, here, pltpu.roll(here, 1, 1))
+        right_side = jnp.where(lane_index == gx - 1, here, pltpu.roll(here, gx - 1, 1))
+        return here + INPLANE_CONDUCT * (down + up + right_side + left_side - 4.0 * here)
+
+    def twin_copy(source, place):
+        return pltpu.make_async_remote_copy(
+            src_ref=twin_out.at[place],
+            dst_ref=twin_in.at[:, slots_of(source % half)],
+            send_sem=twin_send.at[place],
+            recv_sem=twin_recv.at[source % half],
+            device_id=at_sub(ours * PAIR + place),
+            device_id_type=MESH,
+        )
+
+    def heat_from(chip_index):
+        for place in range(PAIR):
+            other = chip_index * PAIR + place
+            heat_copy(other, sub, other).wait_recv()
+
+    heat_from(theirs)
+    border_copy(sub).wait_recv()
+    for count in range(PAIR):
+        place = jnp.where(left, count, PAIR - 1 - count)
+        index = theirs * PAIR + place
+        here = slot_rise[:, rows_of(index)]
+        source, slope = kinetics(
+            conc_in[:, shells - 1, rows_of(index)], here, current_in[:, rows_of(index)]
+        )
+        extra_here = source - slope * here
+        for s in range(slots):
+            first, last = index * rows, index * rows + rows - 1
+            open_low = jnp.logical_and(jnp.logical_not(left), place == 0)
+            open_high = jnp.logical_and(left, place == PAIR - 1)
+            before = slot_rise[s, pl.ds(jnp.where(open_low, first, first - 1), 1)]
+            after = slot_rise[s, pl.ds(jnp.where(open_high, last, last + 1), 1)]
+            rim = border_in[pl.ds(s, 1)]
+            before = jnp.where(open_low, rim, before)
+            after = jnp.where(open_high, rim, after)
+            twin_out[place, 0, s] = smoothed(here[s], before, after) + extra_here[s]
+        twin_out[place, 1] = 1.0 - slope
+        mine_too = sub == ours * PAIR + place
+
+        @pl.when(mine_too)
+        def _():
+            twin_in[:, slots_of(sub % half)] = twin_out[place]
+
+        @pl.when(jnp.logical_not(mine_too))
+        def _():
+            twin_copy(sub, place).start()
+
+    for distance in far:
+        issue(distance, (surf_copy,), jnp.logical_and(outer, jnp.logical_not(left)))
+    for distance in far:
+        issue(distance, (curr_copy,), outer)
 
     @pl.when(sub > 0)
     def _():
@@ -399,30 +500,41 @@
         for copy in face_copies(other, other):
             copy.wait_recv()
 
-    row_index = lax.broadcasted_iota(jnp.int32, (rows, gx), 0)
-    lane_index = lax.broadcasted_iota(jnp.int32, (rows, gx), 1)
-
     def fill(layer, carry):
-        here = heat[0, layer]
-        up = pltpu.roll(here, 1, 0)
-        up = jnp.where(row_index == 0, low_edge[pl.ds(layer, 1)], up)
-        down = pltpu.roll(here, rows - 1, 0)
-        down = jnp.where(row_index == rows - 1, high_edge[pl.ds(layer, 1)], down)
-        left = jnp.where(lane_index == 0, here, pltpu.roll(here, 1, 1))
-        right = jnp.where(lane_index == gx - 1, here, pltpu.roll(here, gx - 1, 1))
-        laplace = down + up + right + left - 4.0 * here
-        base[layer] = here + INPLANE_CONDUCT * laplace
+        base[layer] = smoothed(heat[0, layer], low_edge[pl.ds(layer, 1)], high_edge[pl.ds(layer, 1)])
         return carry
 
     lax.fori_loop(0, layers, fill, jnp.int32(0), unroll=2)
-    lower = contacts[0, cell]
-    upper = contacts[1, cell]
-    below_face = jnp.where(lower >= 0, faces[jnp.maximum(lower, 0), 1], 0.0)
-    above_face = jnp.where(upper >= 0, faces[jnp.maximum(upper, 0), 0], 0.0)
-    base[0] = base[0] + CONTACT_CONDUCT * (below_face - heat[0, 0])
-    base[layers - 1] = base[layers - 1] + CONTACT_CONDUCT * (above_face - heat[0, layers - 1])
-
-    for offset in [0] + arrivals:
+    lower_cell = contacts[0, cell]
+    upper_cell = contacts[1, cell]
+    below_face = jnp.where(lower_cell >= 0, faces[jnp.maximum(lower_cell, 0), 1], 0.0)
+    above_face = jnp.where(upper_cell >= 0, faces[jnp.maximum(upper_cell, 0), 0], 0.0)
+    share = CONTACT_CONDUCT / THROUGH_CONDUCT
+    low_start = share * (below_face - heat[0, 0])
+    high_start = share * (above_face - heat[0, layers - 1])
+    own_start = jnp.where(left, low_start, high_start)
+    other_start = jnp.where(left, high_start, low_start)
+
+    def pair_copy(index, source, target):
+        return pltpu.make_async_remote_copy(
+            src_ref=source,
+            dst_ref=target,
+            send_sem=pair_send.at[index],
+            recv_sem=pair_recv.at[index],
+            device_id=at_sub(twin),
+            device_id_type=MESH,
+        )
+
+    contact_copy = pair_copy(0, contact_out, contact_in)
+    match_copy = pair_copy(1, match_out, match_in)
+    part_copy = pair_copy(2, part, solved.at[pl.ds(own_first, own_slots)])
+
+    @pl.when(middle)
+    def _():
+        contact_out[...] = other_start
+        contact_copy.start()
+
+    def prepare(offset):
         other = partner(sub, offset)
         if offset:
             surf_copy(other, sub, other).wait_recv()
@@ -436,16 +548,119 @@
         extra[at] = source - slope * rise
         diagonal[at] = 1.0 - slope
 
+    def eliminate(bank, low, fetch, start):
+        pivot = jnp.full((rows, gx), 1.0, jnp.float32)
+        before = jnp.full((rows, gx), 0.5, jnp.float32)
+        total = start
+        for step in range(own_slots):
+            index = jnp.where(low, step, own_slots - 1 - step)
+            owner = jnp.where(low, step // slots, subs - 1 - step // slots)
+            filled = jnp.where(low, step % slots, slots - 1 - step % slots) < counts[owner]
+            right, own = fetch(index)
+            own = own + 2.0 * THROUGH_CONDUCT
+            next_pivot = own * pivot - THROUGH_CONDUCT**2 * before
+            next_total = right * pivot + THROUGH_CONDUCT * total
+            inverse = 1.0 / next_pivot
+            factors[bank, step] = jnp.where(filled, THROUGH_CONDUCT * pivot * inverse, 1.0)
+            values[bank, step] = jnp.where(filled, next_total * inverse, 0.0)
+            before = jnp.where(filled, pivot, before)
+            pivot = jnp.where(filled, next_pivot, pivot)
+            total = jnp.where(filled, next_total, total)
+        inverse = 1.0 / pivot
+        return THROUGH_CONDUCT * before * inverse, total * inverse
+
+    def unwind(bank, low, result, target, first):
+        for step in range(own_slots - 1, -1, -1):
+            result = values[bank, step] + factors[bank, step] * result
+            target[first + jnp.where(low, step, own_slots - 1 - step)] = result
+
+    def from_rows(first):
+        def fetch(index):
+            slot = first + index
+            return base[slot_layer[slot]] + extra[slot], diagonal[slot]
+
+        return fetch
+
+    def meeting(factor, value, other_factor, other_value):
+        return (other_value + other_factor * value) / (1.0 - factor * other_factor)
+
+    for offset in [0] + arrivals:
+        if offset < half:
+            prepare(offset)
+    own_factor, own_value = eliminate(0, left, from_rows(own_first), own_start)
+
+    @pl.when(middle)
+    def _():
+        match_out[0] = own_factor
+        match_out[1] = own_value
+        match_copy.start()
+        for place in range(half):
+            source = jnp.where(left, place, half + place)
+
+            @pl.when(source != sub)
+            def _():
+                twin_copy(source, 0).wait_recv()
+
+        contact_copy.wait_recv()
+        factor, value = eliminate(
+            1, left, lambda index: (twin_in[0, index], twin_in[1, index]), contact_in[...]
+        )
+        match_copy.wait_recv()
+        unwind(1, left, meeting(factor, value, match_in[0], match_in[1]), part, 0)
+        part_copy.start()
+
+    for offset in rest:
+        other = partner(sub, offset)
+
+        @pl.when(other // PAIR != theirs)
+        def _():
+            heat_copy(other, sub, other).wait_recv()
+
+        particle(rows_of(other))
+
+    @pl.when(middle)
+    def _():
+        part_copy.wait_recv()
+        rim = solved[jnp.where(left, own_slots, own_slots - slots)]
+        for place in range(1, slots):
+            beyond = solved[jnp.where(left, own_slots, own_slots - slots + place)]
+            rim = jnp.where(counts[half - 1] > place, beyond, rim)
+        unwind(0, left, rim, solved, own_first)
+        contact_copy.wait_send()
+        match_copy.wait_send()
+        part_copy.wait_send()
+
+    @pl.when(jnp.logical_not(middle))
+    def _():
+        for offset in arrivals:
+            if offset >= half:
+                prepare(offset)
+        right = jnp.logical_not(left)
+        factor, value = eliminate(1, right, from_rows(other_first), other_start)
+        across = meeting(own_factor, own_value, factor, value)
+        unwind(0, left, across, solved, own_first)
+        back = meeting(factor, value, own_factor, own_value)
+        unwind(1, right, back, solved, other_first)
+
+    borders(lambda copy: copy.wait_send())
     for layer in range(layers):
-        slot = layer_slot[layer]
-        ends = (layer > 0) + (layer < layers - 1)
-        pivots[layer] = diagonal[slot] + ends * THROUGH_CONDUCT
-        right_side[layer] = base[layer] + extra[slot]
+        answer[0, layer] = solved[layer_slot[layer]]
+
+    for place in range(PAIR):
+
+        @pl.when(sub != ours * PAIR + place)
+        def _():
+            twin_copy(sub, place).wait_send()
 
     for offset in offsets:
         other = partner(sub, offset)
-        for make in (heat_copy, surf_copy, curr_copy):
-            make(sub, other, other).wait_send()
+        heat_copy(sub, other, other).wait_send()
+
+        @pl.when(jnp.logical_or(other // PAIR != theirs, offset < half))
+        def _():
+            surf_copy(sub, other, other).wait_send()
+            curr_copy(sub, other, other).wait_send()
+
     for copy in sends:
         copy.wait_send()
 
@@ -458,45 +673,16 @@
         to_above.wait_send()
 
 
-def finish(conc, right_side, pivots, conc_new, heat_out, heat_new, sem):
+def finish(conc, answer, conc_new, heat_new, sem):
     slots = conc.shape[0]
-    layers = right_side.shape[0]
     writes = [
         pltpu.make_async_copy(conc.at[s], conc_new.at[0, s], sem.at[s]) for s in range(slots)
     ]
+    writes.append(pltpu.make_async_copy(answer, heat_new, sem.at[slots]))
     for write in writes:
         write.start()
-
-    def sweep(order):
-        factors, values = [], []
-        for layer in order:
-            pivot, right = pivots[layer], right_side[layer]
-            if factors:
-                pivot = pivot - THROUGH_CONDUCT * factors[-1]
-                right = right + THROUGH_CONDUCT * values[-1]
-            inverse = 1.0 / pivot
-            factors.append(THROUGH_CONDUCT * inverse)
-            values.append(right * inverse)
-        return factors, values
-
-    middle = layers // 2
-    low_f, low_v = sweep(range(middle))
-    high_f, high_v = sweep(range(layers - 1, middle - 1, -1))
-    low = (low_v[-1] + low_f[-1] * high_v[-1]) / (1.0 - low_f[-1] * high_f[-1])
-    high = high_v[-1] + high_f[-1] * low
-    heat_new[0, middle - 1] = low
-    heat_new[0, middle] = high
-    for step in range(middle - 2, -1, -1):
-        low = low_v[step] + low_f[step] * low
-        heat_new[0, step] = low
-    for step in range(len(high_v) - 2, -1, -1):
-        high = high_v[step] + high_f[step] * high
-        heat_new[0, layers - 1 - step] = high
-    heat_write = pltpu.make_async_copy(heat_new, heat_out, sem.at[slots])
-    heat_write.start()
     for write in writes:
         write.wait()
-    heat_write.wait()
 
 
 def per_device(cells, subs, shell_conc, heat_rise, layer_current, layer_counts, contacts):
@@ -505,21 +691,21 @@
     f32 = jnp.float32
     dma = pltpu.SemaphoreType.DMA
     table = (layers, rows, gx)
+    own_slots = subs // 2 * slots
     held = [
         pltpu.with_memory_space_constraint(array, pltpu.HBM)
         for array in (layer_counts, contacts.T, heat_rise, shell_conc, layer_current)
     ]
-    conc, right_side, pivots = pl.pallas_call(
+    conc, answer = pl.pallas_call(
         functools.partial(kernel, cells, subs),
         out_shape=(
             pltpu.VMEM((slots, shells, gy, gx), f32),
-            pltpu.VMEM(table, f32),
-            pltpu.VMEM(table, f32),
+            pltpu.VMEM(heat_rise.shape, f32),
         ),
         in_specs=[
             pl.BlockSpec(memory_space=pltpu.HBM)
         ] * 5,
-        out_specs=(pl.BlockSpec(memory_space=pltpu.VMEM),) * 3,
+        out_specs=(pl.BlockSpec(memory_space=pltpu.VMEM),) * 2,
         scratch_shapes=[
             pltpu.VMEM(heat_rise.shape, f32),
             pltpu.VMEM((subs * slots, rows, gx), f32),
@@ -535,8 +721,21 @@
             pltpu.VMEM((subs * slots, rows, gx), f32),
             pltpu.VMEM((subs * slots, rows, gx), f32),
             pltpu.SMEM((layers,), jnp.int32),
+            pltpu.SMEM((subs * slots,), jnp.int32),
             pltpu.SMEM(layer_counts.shape, jnp.int32),
             pltpu.SMEM(contacts.shape[::-1], jnp.int32),
+            pltpu.VMEM((PAIR, 2, slots, rows, gx), f32),
+            pltpu.VMEM((2, own_slots, rows, gx), f32),
+            pltpu.VMEM((subs * slots, rows, gx), f32),
+            pltpu.VMEM((2, own_slots, rows, gx), f32),
+            pltpu.VMEM((2, own_slots, rows, gx), f32),
+            pltpu.VMEM((rows, gx), f32),
+            pltpu.VMEM((rows, gx), f32),
+            pltpu.VMEM((2, rows, gx), f32),
+            pltpu.VMEM((2, rows, gx), f32),
+            pltpu.VMEM((own_slots, rows, gx), f32),
+            pltpu.VMEM((subs, slots, gx), f32),
+            pltpu.VMEM((slots, gx), f32),
             pltpu.SemaphoreType.REGULAR((2, max(subs // PAIR, 2))),
             pltpu.SemaphoreType.REGULAR((2, max(cells.bit_length() - 1, 1))),
             dma((7,)),
@@ -550,6 +749,12 @@
             dma((2,)),
             dma((2 * cells,)),
             dma((2 * cells,)),
+            dma((PAIR,)),
+            dma((subs // 2,)),
+            dma((3,)),
+            dma((3,)),
+            dma((subs,)),
+            dma((1,)),
         ],
         compiler_params=pltpu.CompilerParams(
             collective_id=0, has_side_effects=True, vmem_limit_bytes=GRANT
@@ -561,14 +766,14 @@
             jax.ShapeDtypeStruct(shell_conc.shape, f32),
             jax.ShapeDtypeStruct(heat_rise.shape, f32),
         ),
-        in_specs=[pl.BlockSpec(memory_space=pltpu.VMEM)] * 3,
+        in_specs=[pl.BlockSpec(memory_space=pltpu.VMEM)] * 2,
         out_specs=(
             pl.BlockSpec(memory_space=pl.ANY),
             pl.BlockSpec(memory_space=pl.ANY),
         ),
-        scratch_shapes=[pltpu.VMEM(heat_rise.shape, f32), dma((slots + 1,))],
+        scratch_shapes=[dma((slots + 1,))],
         compiler_params=pltpu.CompilerParams(vmem_limit_bytes=GRANT),
-    )(conc, right_side, pivots)
+    )(conc, answer)
     return conc_new, heat_new
 
 

time: 24.1 us -> 23.5 us (0.975)
  the two profiles are of different devices: /device:TPU:9 before, /device:TPU:10 now
where the time goes in v3:
time: 23.5 us; the launch traced here: 23.4 us
  Pallas kernels  22.8 us (97%)
  between operations  0.64 us (3%)
    pallas_call x1, Pallas kernels, per_device(): pl.pallas_call(functools.partial(kernel, cells, subs), out_shape=(pltpu.V...  21.2 us
    pallas_call x1, Pallas kernels, per_device(): pl.pallas_call(finish, out_shape=(jax.ShapeDtypeStruct(shell_conc.shape,...  1.6 us

profile of v3, /device:TPU:10, one launch (start us, length us, event | category | flops | bytes accessed | tf_op | source)
XLA Modules:
  0.0 23.4 jit_solution(706443980635770319)
XLA Ops:
  0.6 21.2 %shard_map.68 = (f32[4,10,128,128]{3,2,1,0:T(8,128)S(1)}, f32[1,30,16,128]{3,2,1,0:T(8,128)S(1)}) custom-call(s32[8]{0:T(128)} %counts_hbm.1, s32[2,4]{1,0:T(2,128)} %bitcast.1, f32[1,30,16,128]{3,2,1,0:T(8,128)} %heat_hbm.1, f32[1,4,10,128,128]{4,3,2,1,0:T(8,128)} %conc.1, f32[1,4,128,128]{3,2,1,0:T(8,128)} %current.1), custom_call_target="tpu_custom_call" | custom-call | tf_op jit(solution)/shard_map/pallas_call | solution.py:699
  21.8 1.6 %shard_map.69 = (f32[1,4,10,128,128]{4,3,2,1,0:T(8,128)}, f32[1,30,16,128]{3,2,1,0:T(8,128)}) custom-call(f32[4,10,128,128]{3,2,1,0:T(8,128)S(1)} %get-tuple-element.4.conc, f32[1,30,16,128]{3,2,1,0:T(8,128)S(1)} %get-tuple-element.5.answer), custom_call_target="tpu_custom_call" | custom-call | tf_op jit(solution)/shard_map/pallas_call | solution.py:763

commit v4 on v3

--- a/solution.py
+++ b/solution.py
@@ -307,9 +307,9 @@
     for distance in far:
         issue(distance, (heat_copy,))
     for distance in far:
-        issue(distance, (surf_copy, curr_copy), inner)
+        issue(distance, (surf_copy,), inner)
     for distance in far:
-        issue(distance, (surf_copy,), jnp.logical_and(outer, left))
+        issue(distance, (surf_copy,), outer)
 
     def face_copies(source, device):
         return [
@@ -475,7 +475,7 @@
             twin_copy(sub, place).start()
 
     for distance in far:
-        issue(distance, (surf_copy,), jnp.logical_and(outer, jnp.logical_not(left)))
+        issue(distance, (curr_copy,), inner)
     for distance in far:
         issue(distance, (curr_copy,), outer)
 

time: 23.5 us -> 23.5 us (level)
  no operation moved by 1% of the time
where the time goes in v4:
time: 23.5 us; the launch traced here: 23.4 us
  Pallas kernels  22.7 us (97%)
  between operations  0.64 us (3%)
    pallas_call x1, Pallas kernels, per_device(): pl.pallas_call(functools.partial(kernel, cells, subs), out_shape=(pltpu.V...  21.1 us
    pallas_call x1, Pallas kernels, per_device(): pl.pallas_call(finish, out_shape=(jax.ShapeDtypeStruct(shell_conc.shape,...  1.6 us

profile of v4, /device:TPU:10, one launch (start us, length us, event | category | flops | bytes accessed | tf_op | source)
XLA Modules:
  0.0 23.4 jit_solution(6756258634299666749)
XLA Ops:
  0.6 21.1 %shard_map.68 = (f32[4,10,128,128]{3,2,1,0:T(8,128)S(1)}, f32[1,30,16,128]{3,2,1,0:T(8,128)S(1)}) custom-call(s32[8]{0:T(128)} %counts_hbm.1, s32[2,4]{1,0:T(2,128)} %bitcast.1, f32[1,30,16,128]{3,2,1,0:T(8,128)} %heat_hbm.1, f32[1,4,10,128,128]{4,3,2,1,0:T(8,128)} %conc.1, f32[1,4,128,128]{3,2,1,0:T(8,128)} %current.1), custom_call_target="tpu_custom_call" | custom-call | tf_op jit(solution)/shard_map/pallas_call | solution.py:699
  21.8 1.6 %shard_map.69 = (f32[1,4,10,128,128]{4,3,2,1,0:T(8,128)}, f32[1,30,16,128]{3,2,1,0:T(8,128)}) custom-call(f32[4,10,128,128]{3,2,1,0:T(8,128)S(1)} %get-tuple-element.4.conc, f32[1,30,16,128]{3,2,1,0:T(8,128)S(1)} %get-tuple-element.5.answer), custom_call_target="tpu_custom_call" | custom-call | tf_op jit(solution)/shard_map/pallas_call | solution.py:763

commit v5 on v4

--- a/solution.py
+++ b/solution.py
@@ -231,7 +231,7 @@
                         other = on_chip(shift, place if distance else (core + place) % PAIR)
                         make(sub, other, other).start()
 
-    issue(1, (curr_copy, surf_copy), outer)
+    issue(1, (curr_copy,), outer)
     for load in first_loads:
         load.wait()
     edges[0] = heat[0, :, 0]
@@ -252,6 +252,7 @@
     if chips > 2:
         relay(2)
     issue(1, (heat_copy,), within=False)
+    issue(1, (surf_copy,), outer)
     issue(0, (heat_copy, surf_copy, curr_copy))
     to_below = pltpu.make_async_remote_copy(
         src_ref=edges.at[0],

time: 23.5 us -> 23.5 us (level)
  no operation moved by 1% of the time
where the time goes in v5:
time: 23.5 us; the launch traced here: 23.4 us
  Pallas kernels  22.8 us (97%)
  between operations  0.64 us (3%)
    pallas_call x1, Pallas kernels, per_device(): pl.pallas_call(functools.partial(kernel, cells, subs), out_shape=(pltpu.V...  21.2 us
    pallas_call x1, Pallas kernels, per_device(): pl.pallas_call(finish, out_shape=(jax.ShapeDtypeStruct(shell_conc.shape,...  1.6 us

profile of v5, /device:TPU:10, one launch (start us, length us, event | category | flops | bytes accessed | tf_op | source)
XLA Modules:
  0.0 23.4 jit_solution(3239876655541543982)
XLA Ops:
  0.6 21.2 %shard_map.68 = (f32[4,10,128,128]{3,2,1,0:T(8,128)S(1)}, f32[1,30,16,128]{3,2,1,0:T(8,128)S(1)}) custom-call(s32[8]{0:T(128)} %counts_hbm.1, s32[2,4]{1,0:T(2,128)} %bitcast.1, f32[1,30,16,128]{3,2,1,0:T(8,128)} %heat_hbm.1, f32[1,4,10,128,128]{4,3,2,1,0:T(8,128)} %conc.1, f32[1,4,128,128]{3,2,1,0:T(8,128)} %current.1), custom_call_target="tpu_custom_call" | custom-call | tf_op jit(solution)/shard_map/pallas_call | solution.py:700
  21.8 1.6 %shard_map.69 = (f32[1,4,10,128,128]{4,3,2,1,0:T(8,128)}, f32[1,30,16,128]{3,2,1,0:T(8,128)}) custom-call(f32[4,10,128,128]{3,2,1,0:T(8,128)S(1)} %get-tuple-element.4.conc, f32[1,30,16,128]{3,2,1,0:T(8,128)S(1)} %get-tuple-element.5.answer), custom_call_target="tpu_custom_call" | custom-call | tf_op jit(solution)/shard_map/pallas_call | solution.py:764
